TPU v7x, 256 devices: a whole 4x4x8 slice. The times are simulated.
256 devices in a mesh: row: 16 (over x_hi, z), col: 16 (over y, x_lo, core).
Axes of the slice: x: 4 (x_hi: 2, x_lo: 2; x = x_hi * 2 + x_lo), y: 4, z: 8, core: 2. Of those that a mesh axis runs over, the one named last changes fastest.
Arguments:
- node_feats: bfloat16 [65536, 256], P(('row', 'col')), may hold values from -6 to 6
- dest_grad: bfloat16 [16, 4096, 256], P('col', 'row'), may hold values from -6 to 6
- bases: bfloat16 [30, 256, 256], replicated, may hold values from -0.375 to 0.375
- coefs: bfloat16 [2000, 30], replicated, may hold values from -1 to 1
- src_ids: int32 [16, 16, 1024], P('row', 'col'), may hold values from 0 to 4095
- dst_ids: int32 [16, 16, 1024], P('row', 'col'), may hold values from 0 to 4095
- rel_ids: int32 [16, 16, 1024], P('row', 'col'), may hold values from 0 to 1999
- edge_norm: float32 [16, 16, 1024], P('row', 'col'), may hold values from 0.1 to 1
- block_fill: int32 [16, 16, 8], P('row', 'col'), may hold values from 0 to 128, as said below
Outputs:
- node_grad: bfloat16 [65536, 256], P(('row', 'col'))
- basis_grad: float32 [7680, 256], P(('row', 'col'))
- coef_grad: float32 [2000, 30], replicated
Inputs may be any that keep to these rules, and one draw needn't show every extreme that they name: `block_fill`: the first block of every device is full, and blocks after a device's last live block are empty.
All inputs are finite; a program needn't handle non-finite values.
Results may differ from a plain program's by a relative error of at most 0.0049.
Values may be sent and summed in bfloat16 or wider, within the bound.
A program may use at most 64 MiB of HBM per device.

v0:
```python
import jax
import jax.numpy as jnp
from jax import lax
from jax.sharding import PartitionSpec as P

EDGE_BLOCK = 128


def on_device(
    node_feats, dest_grad, bases, coefs, src_ids, dst_ids, rel_ids, edge_norm, block_fill
):
    col_count = lax.axis_size("col")
    source_rows = lax.all_gather(node_feats, "col", axis=0, tiled=True)
    target_rows = lax.all_gather(dest_grad[0], "row", axis=0, tiled=True)
    sources = src_ids.reshape(-1)
    targets = dst_ids.reshape(-1)
    relations = rel_ids.reshape(-1)
    fills = block_fill.reshape(-1)
    block_total = fills.shape[0]
    position = lax.broadcasted_iota(jnp.int32, (block_total, EDGE_BLOCK), 1)
    live_mask = (position < fills[:, None]).reshape(-1).astype(jnp.float32)
    weights = edge_norm.reshape(-1) * live_mask
    edge_total = sources.shape[0]
    edge_grad = (weights[:, None] * target_rows[targets].astype(jnp.float32)).astype(jnp.bfloat16)
    edge_rows = source_rows[sources]
    edge_coefs = coefs[relations]
    basis_count = bases.shape[0]
    width = bases.shape[1]
    vertex_count = source_rows.shape[0]
    relation_count = coefs.shape[0]
    block_span = 512
    node_part = jnp.zeros((vertex_count, width), jnp.float32)
    coef_part = jnp.zeros((relation_count, basis_count), jnp.float32)
    for offset in range(0, edge_total, block_span):
        grad_block = edge_grad[offset : offset + block_span]
        rows_block = edge_rows[offset : offset + block_span]
        coef_block = edge_coefs[offset : offset + block_span].astype(jnp.float32)
        backed = lax.dot_general(
            grad_block, bases, (((1,), (2,)), ((), ())), preferred_element_type=jnp.float32
        )
        per_edge = jnp.sum(coef_block[:, :, None] * backed, axis=1)
        inner = jnp.sum(backed * rows_block[:, None, :].astype(jnp.float32), axis=2)
        node_part = node_part + jax.ops.segment_sum(
            per_edge, sources[offset : offset + block_span], num_segments=vertex_count
        )
        coef_part = coef_part + jax.ops.segment_sum(
            inner, relations[offset : offset + block_span], num_segments=relation_count
        )
    node_grad = lax.psum_scatter(node_part, "col", scatter_dimension=0, tiled=True).astype(
        jnp.bfloat16
    )
    basis_rows = (edge_coefs[:, :, None] * edge_rows[:, None, :]).reshape(
        edge_total, basis_count * width
    )
    basis_grad = lax.psum_scatter(
        lax.dot_general(
            basis_rows, edge_grad, (((0,), (0,)), ((), ())), preferred_element_type=jnp.float32
        ),
        ("row", "col"),
        scatter_dimension=0,
        tiled=True,
    )
    coef_grad = lax.psum(coef_part, ("row", "col"))
    return (node_grad, basis_grad / col_count, coef_grad / col_count)


def solution(mesh):
    in_specs = (
        P(("row", "col"), None),
        P("col", "row", None),
        P(),
        P(),
        P("row", "col", None),
        P("row", "col", None),
        P("row", "col", None),
        P("row", "col", None),
        P("row", "col", None),
    )
    out_specs = (P(("row", "col"), None), P(("row", "col"), None), P())
    return jax.shard_map(
        on_device, mesh=mesh, in_specs=in_specs, out_specs=out_specs, check_vma=False
    )
```

profile of v0, /device:TPU:4, one launch (start us, length us, event | category | flops | bytes accessed | tf_op | source)
XLA Modules:
  0.0 924.1 jit_solution(12984734901086320531)
XLA Ops:
  10.6 3.2 gather_fusion
  17.6 31.2 %all-gather.4.cloned.1.call-done = bf16[4096,256]{1,0:T(8,128)(2,1)} async-done(((bf16[256,256]{1,0:T(8,128)(2,1)}), bf16[4096,256]{1,0:T(8,128)(2,1)}) %all-gather.4.cloned.1.call-update) | async-done | bytes 2097168 | tf_op jit(solution)/shard_map/all_gather | solution.py:13
  48.8 5.3 gather_fusion.2
  54.6 80.1 %all-gather.6.cloned.1.call-done = bf16[1,4096,256]{2,1,0:T(8,128)(2,1)} async-done(((bf16[1,256,256]{2,1,0:T(8,128)(2,1)}), bf16[1,4096,256]{2,1,0:T(8,128)(2,1)}) %all-gather.6.cloned.1.call-update) | async-done | bytes 2097168 | tf_op jit(solution)/shard_map/all_gather | solution.py:14
  134.7 5.3 gather_fusion.1
  140.2 6.3 multiply_reduce_fusion
  146.5 4.2 multiply_reduce_fusion.1
  151.0 7.0 scatter_custom_fusion.1
  159.7 8.3 scatter_custom_fusion
  168.2 4.1 broadcast_multiply_fusion
  172.3 6.7 fusion.9
  179.0 597.6 %fusion = f32[32,256]{1,0:T(8,128)S(1)} fusion(f32[7680,256]{1,0:T(8,128)} %fusion.9), kind=kCustom, calls=%all-reduce-scatter | all-reduce-scatter fusion | flops 2097153 | bytes 7897088
  776.6 1.9 collective-permute-start.15
  778.6 1.9 collective-permute-start.14
  780.5 1.9 collective-permute-start.13
  782.4 1.9 collective-permute-start.12
  784.3 1.9 collective-permute-start.11
  786.3 6.7 collective-permute-start.10
  793.0 8.1 collective-permute-start.9
  801.1 1.9 collective-permute-start.8
  803.1 14.8 %collective-permute-start.7 = (f32[32,256]{1,0:T(8,128)S(1)}, f32[32,256]{1,0:T(8,128)S(1)}, u32[]{:S(2)}, u32[]{:S(2)}) collective-permute-start(f32[32,256]{1,0:T(8,128)S(1)} %fusion), channel_id=1, source_target_pairs={{0,8},{1,9},{2,10},{3,11},{4,12},{5,13},{6,14},{7,15},{8,16},{9,17... | collective-permute-start | bytes 98312
  817.9 27.8 %collective-permute-start.6 = (f32[32,256]{1,0:T(8,128)S(1)}, f32[32,256]{1,0:T(8,128)S(1)}, u32[]{:S(2)}, u32[]{:S(2)}) collective-permute-start(f32[32,256]{1,0:T(8,128)S(1)} %fusion), channel_id=1, source_target_pairs={{0,7},{1,8},{2,9},{3,10},{4,11},{5,12},{6,13},{7,14},{8,15},{9,16}... | collective-permute-start | bytes 98312
  845.8 24.3 %collective-permute-start.5 = (f32[32,256]{1,0:T(8,128)S(1)}, f32[32,256]{1,0:T(8,128)S(1)}, u32[]{:S(2)}, u32[]{:S(2)}) collective-permute-start(f32[32,256]{1,0:T(8,128)S(1)} %fusion), channel_id=1, source_target_pairs={{0,6},{1,7},{2,8},{3,9},{4,10},{5,11},{6,12},{7,13},{8,14},{9,15},... | collective-permute-start | bytes 98312
  870.1 17.0 %collective-permute-start.4 = (f32[32,256]{1,0:T(8,128)S(1)}, f32[32,256]{1,0:T(8,128)S(1)}, u32[]{:S(2)}, u32[]{:S(2)}) collective-permute-start(f32[32,256]{1,0:T(8,128)S(1)} %fusion), channel_id=1, source_target_pairs={{0,5},{1,6},{2,7},{3,8},{4,9},{5,10},{6,11},{7,12},{8,13},{9,14},{... | collective-permute-start | bytes 98312
  887.1 2.5 collective-permute-start.3
  889.6 8.7 collective-permute-start.2
  898.3 3.0 collective-permute-start.1
  901.4 1.9 collective-permute-start
  903.4 3.7 collective-permute-done.2
  908.4 2.5 collective-permute-done
  910.9 2.1 concatenate.16
  915.9 1.6 convert_element_type.28
  (53 shorter events, 14.2 us)
Async XLA Ops:
  7.2 41.6 %all-gather.4.cloned.1.call-start = ((), (), s32[]{:S(2)}) async-start(), calls=%async_computation.2 | async-start | bytes 2228224 | tf_op jit(solution)/shard_map/all_gather | solution.py:13
  7.9 126.8 %all-gather.6.cloned.1.call-start = ((), (), s32[]{:S(2)}) async-start(), calls=%async_computation.4 | async-start | bytes 2228224 | tf_op jit(solution)/shard_map/all_gather | solution.py:14
  8.6 904.9 %all-reduce.4.cloned.1.call-start = ((), (), s32[]{:S(2)}) async-start(), calls=%async_computation.3 | async-start | bytes 2048000 | tf_op jit(solution)/shard_map/psum | solution.py:63
  140.2 6.3 copy-start
  158.0 757.9 %reduce-scatter.4.cloned.1.call-start = ((), (), s32[]{:S(2)}) async-start(), calls=%async_computation.1 | async-start | bytes 4456448 | tf_op jit(solution)/shard_map/reduce_scatter | solution.py:49
  776.6 9.6 %collective-permute-start.15 = (f32[30,256]{1,0:T(8,128)S(1)}, f32[30,256]{1,0:T(8,128)S(1)}, u32[]{:S(2)}, u32[]{:S(2)}) collective-permute-start(f32[30,256]{1,0:T(8,128)S(1)} %slice.56), channel_id=1, source_target_pairs={{0,16},{1,17},{2,18},{3,19},{4,20},{5,21},{6,22},{7,23},{8,24},{9,... | collective-permute-start | bytes 92168
  778.6 14.5 %collective-permute-start.14 = (f32[32,256]{1,0:T(8,128)S(1)}, f32[32,256]{1,0:T(8,128)S(1)}, u32[]{:S(2)}, u32[]{:S(2)}) collective-permute-start(f32[32,256]{1,0:T(8,128)S(1)} %fusion), channel_id=1, source_target_pairs={{0,15},{1,16},{2,17},{3,18},{4,19},{5,20},{6,21},{7,22},{8,23},{9,... | collective-permute-start | bytes 98312
  780.5 20.6 %collective-permute-start.13 = (f32[32,256]{1,0:T(8,128)S(1)}, f32[32,256]{1,0:T(8,128)S(1)}, u32[]{:S(2)}, u32[]{:S(2)}) collective-permute-start(f32[32,256]{1,0:T(8,128)S(1)} %fusion), channel_id=1, source_target_pairs={{0,14},{1,15},{2,16},{3,17},{4,18},{5,19},{6,20},{7,21},{8,22},{9,... | collective-permute-start | bytes 98312
  782.4 20.6 %collective-permute-start.12 = (f32[32,256]{1,0:T(8,128)S(1)}, f32[32,256]{1,0:T(8,128)S(1)}, u32[]{:S(2)}, u32[]{:S(2)}) collective-permute-start(f32[32,256]{1,0:T(8,128)S(1)} %fusion), channel_id=1, source_target_pairs={{0,13},{1,14},{2,15},{3,16},{4,17},{5,18},{6,19},{7,20},{8,21},{9,... | collective-permute-start | bytes 98312
  784.3 33.6 %collective-permute-start.11 = (f32[32,256]{1,0:T(8,128)S(1)}, f32[32,256]{1,0:T(8,128)S(1)}, u32[]{:S(2)}, u32[]{:S(2)}) collective-permute-start(f32[32,256]{1,0:T(8,128)S(1)} %fusion), channel_id=1, source_target_pairs={{0,12},{1,13},{2,14},{3,15},{4,16},{5,17},{6,18},{7,19},{8,20},{9,... | collective-permute-start | bytes 98312
  786.3 59.5 %collective-permute-start.10 = (f32[32,256]{1,0:T(8,128)S(1)}, f32[32,256]{1,0:T(8,128)S(1)}, u32[]{:S(2)}, u32[]{:S(2)}) collective-permute-start(f32[32,256]{1,0:T(8,128)S(1)} %fusion), channel_id=1, source_target_pairs={{0,11},{1,12},{2,13},{3,14},{4,15},{5,16},{6,17},{7,18},{8,19},{9,... | collective-permute-start | bytes 98312
  793.0 77.1 %collective-permute-start.9 = (f32[32,256]{1,0:T(8,128)S(1)}, f32[32,256]{1,0:T(8,128)S(1)}, u32[]{:S(2)}, u32[]{:S(2)}) collective-permute-start(f32[32,256]{1,0:T(8,128)S(1)} %fusion), channel_id=1, source_target_pairs={{0,10},{1,11},{2,12},{3,13},{4,14},{5,15},{6,16},{7,17},{8,18},{9,... | collective-permute-start | bytes 98312
  801.1 86.0 %collective-permute-start.8 = (f32[32,256]{1,0:T(8,128)S(1)}, f32[32,256]{1,0:T(8,128)S(1)}, u32[]{:S(2)}, u32[]{:S(2)}) collective-permute-start(f32[32,256]{1,0:T(8,128)S(1)} %fusion), channel_id=1, source_target_pairs={{0,9},{1,10},{2,11},{3,12},{4,13},{5,14},{6,15},{7,16},{8,17},{9,1... | collective-permute-start | bytes 98312
  803.1 86.6 %collective-permute-start.7 = (f32[32,256]{1,0:T(8,128)S(1)}, f32[32,256]{1,0:T(8,128)S(1)}, u32[]{:S(2)}, u32[]{:S(2)}) collective-permute-start(f32[32,256]{1,0:T(8,128)S(1)} %fusion), channel_id=1, source_target_pairs={{0,8},{1,9},{2,10},{3,11},{4,12},{5,13},{6,14},{7,15},{8,16},{9,17... | collective-permute-start | bytes 98312
  817.9 80.4 %collective-permute-start.6 = (f32[32,256]{1,0:T(8,128)S(1)}, f32[32,256]{1,0:T(8,128)S(1)}, u32[]{:S(2)}, u32[]{:S(2)}) collective-permute-start(f32[32,256]{1,0:T(8,128)S(1)} %fusion), channel_id=1, source_target_pairs={{0,7},{1,8},{2,9},{3,10},{4,11},{5,12},{6,13},{7,14},{8,15},{9,16}... | collective-permute-start | bytes 98312
  845.8 55.6 %collective-permute-start.5 = (f32[32,256]{1,0:T(8,128)S(1)}, f32[32,256]{1,0:T(8,128)S(1)}, u32[]{:S(2)}, u32[]{:S(2)}) collective-permute-start(f32[32,256]{1,0:T(8,128)S(1)} %fusion), channel_id=1, source_target_pairs={{0,6},{1,7},{2,8},{3,9},{4,10},{5,11},{6,12},{7,13},{8,14},{9,15},... | collective-permute-start | bytes 98312
  870.1 33.2 %collective-permute-start.4 = (f32[32,256]{1,0:T(8,128)S(1)}, f32[32,256]{1,0:T(8,128)S(1)}, u32[]{:S(2)}, u32[]{:S(2)}) collective-permute-start(f32[32,256]{1,0:T(8,128)S(1)} %fusion), channel_id=1, source_target_pairs={{0,5},{1,6},{2,7},{3,8},{4,9},{5,10},{6,11},{7,12},{8,13},{9,14},{... | collective-permute-start | bytes 98312
  887.1 16.3 %collective-permute-start.3 = (f32[32,256]{1,0:T(8,128)S(1)}, f32[32,256]{1,0:T(8,128)S(1)}, u32[]{:S(2)}, u32[]{:S(2)}) collective-permute-start(f32[32,256]{1,0:T(8,128)S(1)} %fusion), channel_id=1, source_target_pairs={{0,4},{1,5},{2,6},{3,7},{4,8},{5,9},{6,10},{7,11},{8,12},{9,13},{1... | collective-permute-start | bytes 98312
  889.6 17.5 %collective-permute-start.2 = (f32[32,256]{1,0:T(8,128)S(1)}, f32[32,256]{1,0:T(8,128)S(1)}, u32[]{:S(2)}, u32[]{:S(2)}) collective-permute-start(f32[32,256]{1,0:T(8,128)S(1)} %fusion), channel_id=1, source_target_pairs={{0,3},{1,4},{2,5},{3,6},{4,7},{5,8},{6,9},{7,10},{8,11},{9,12},{10... | collective-permute-start | bytes 98312
  898.3 10.0 %collective-permute-start.1 = (f32[32,256]{1,0:T(8,128)S(1)}, f32[32,256]{1,0:T(8,128)S(1)}, u32[]{:S(2)}, u32[]{:S(2)}) collective-permute-start(f32[32,256]{1,0:T(8,128)S(1)} %fusion), channel_id=1, source_target_pairs={{0,2},{1,3},{2,4},{3,5},{4,6},{5,7},{6,8},{7,9},{8,10},{9,11},{10,... | collective-permute-start | bytes 98312
  901.4 9.5 %collective-permute-start = (f32[32,256]{1,0:T(8,128)S(1)}, f32[32,256]{1,0:T(8,128)S(1)}, u32[]{:S(2)}, u32[]{:S(2)}) collective-permute-start(f32[32,256]{1,0:T(8,128)S(1)} %fusion), channel_id=1, source_target_pairs={{0,1},{1,2},{2,3},{3,4},{4,5},{5,6},{6,7},{7,8},{8,9},{9,10},{10,1... | collective-permute-start | bytes 98312
Sparse Core Ops, SparseCore 0:
  9.8 38.8 all-gather.3
  51.3 83.2 all-gather.5
  158.1 258.4 all-reduce.3
  419.0 74.0 reduce-scatter.3
where the time goes:
time: 925 us; the launch traced here: 924 us
  blocking collectives  598 us (65%)
  starting transfers between devices  127 us (14%)
  waiting for transfers between devices  120 us (13%)
  other arithmetic  27.4 us (3%)
  local copies, waits for them, and re-layouts  20.9 us (2%)
  matrix products  17.1 us (2%)
  between operations  14.1 us (2%)
    unnamed x1, blocking collectives  598 us
    unnamed x16, starting transfers between devices  126 us
    all_gather x1, waiting for transfers between devices, on_device(): target_rows = lax.all_gather(dest_grad[0], 'row', axis=0, tiled=True)  80.1 us
    all_gather x1, waiting for transfers between devices, on_device(): source_rows = lax.all_gather(node_feats, 'col', axis=0, tiled=True)  31.2 us
  transfers between devices with their start and end apart: 20, of which 5 were waited for; matrix products, arithmetic and copies ran while one was open for 69% of the time, Pallas kernels for 0%

commit v1 on v0

--- a/solution.py
+++ b/solution.py
@@ -6,12 +6,19 @@
 EDGE_BLOCK = 128
 
 
+def gather_over(x, name, dim):
+    n_dev = lax.axis_size(name)
+    blocks = jnp.stack([x for _ in range(n_dev)])
+    blocks = lax.all_to_all(blocks, name, split_axis=0, concat_axis=0)
+    return jnp.concatenate(blocks, axis=dim)
+
+
 def on_device(
     node_feats, dest_grad, bases, coefs, src_ids, dst_ids, rel_ids, edge_norm, block_fill
 ):
     col_count = lax.axis_size("col")
     source_rows = lax.all_gather(node_feats, "col", axis=0, tiled=True)
-    target_rows = lax.all_gather(dest_grad[0], "row", axis=0, tiled=True)
+    target_rows = gather_over(dest_grad[0], "row", 0)
     sources = src_ids.reshape(-1)
     targets = dst_ids.reshape(-1)
     relations = rel_ids.reshape(-1)

time: 925 us -> 856 us (0.925)
  waiting for transfers between devices: 120 us -> 42.2 us
  starting transfers between devices: 127 us -> 138 us
    all_gather x1 -> x0, waiting for transfers between devices: 80.1 us -> none  [on_device(): target_rows = lax.all_gather(dest_grad[0], 'row', axis=0, tiled=True)]
    all_to_all x0 -> x1, starting transfers between devices: none -> 11.4 us  [gather_over(): blocks = lax.all_to_all(blocks, name, split_axis=0, concat_axis=0)]
  transfers between devices with their start and end apart: 20 -> 20, of which waited for: 5 -> 5; matrix products, arithmetic and copies ran while one was open for 69% -> 75% of each run, Pallas kernels for 0% -> 0%
where the time goes in v1:
time: 856 us; the launch traced here: 855 us
  blocking collectives  597 us (70%)
  starting transfers between devices  138 us (16%)
  waiting for transfers between devices  42.2 us (5%)
  other arithmetic  24.9 us (3%)
  local copies, waits for them, and re-layouts  23.3 us (3%)
  matrix products  15.6 us (2%)
  between operations  14.3 us (2%)
    unnamed x1, blocking collectives  597 us
    unnamed x16, starting transfers between devices  126 us
    all_gather x1, waiting for transfers between devices, on_device(): source_rows = lax.all_gather(node_feats, 'col', axis=0, tiled=True)  28.5 us
  transfers between devices with their start and end apart: 20, of which 5 were waited for; matrix products, arithmetic and copies ran while one was open for 75% of the time, Pallas kernels for 0%

profile of v1, /device:TPU:4, one launch (start us, length us, event | category | flops | bytes accessed | tf_op | source)
XLA Modules:
  0.0 855.2 jit_solution(10719383880357969187)
XLA Ops:
  8.0 2.4 stack.3
  10.4 11.4 %all-to-all-start = ((bf16[16,256,256]{2,1,0:T(8,128)(2,1)}), bf16[16,256,256]{2,1,0:T(8,128)(2,1)S(1)}, u32[]{:S(2)}, u32[]{:S(2)}) async-start(bf16[16,256,256]{2,1,0:T(8,128)(2,1)} %stack.3), calls=%async_computation | async-start | bytes 4194304 | tf_op jit(solution)/shard_map/all_to_all | solution.py:12
  23.8 3.2 gather_fusion
  27.4 28.5 %all-gather.2.cloned.1.call-done = bf16[4096,256]{1,0:T(8,128)(2,1)} async-done(((bf16[256,256]{1,0:T(8,128)(2,1)}), bf16[4096,256]{1,0:T(8,128)(2,1)}) %all-gather.2.cloned.1.call-update) | async-done | bytes 2097168 | tf_op jit(solution)/shard_map/all_gather | solution.py:20
  55.9 5.3 gather_fusion.2
  62.1 2.0 copy.42
  65.1 5.5 all-to-all-done
  70.7 3.9 gather_fusion.1
  74.9 5.5 multiply_reduce_fusion
  80.4 3.4 multiply_reduce_fusion.1
  84.1 7.0 scatter_custom_fusion.1
  91.6 8.3 scatter_custom_fusion
  100.1 4.1 broadcast_multiply_fusion
  104.2 6.6 fusion.9
  110.9 597.2 %fusion = f32[32,256]{1,0:T(8,128)S(1)} fusion(f32[7680,256]{1,0:T(8,128)} %fusion.9), kind=kCustom, calls=%all-reduce-scatter | all-reduce-scatter fusion | flops 2097153 | bytes 7897088
  708.1 1.9 collective-permute-start.15
  710.0 1.9 collective-permute-start.14
  712.0 1.9 collective-permute-start.13
  713.9 1.9 collective-permute-start.12
  715.8 1.9 collective-permute-start.11
  717.8 8.0 collective-permute-start.10
  725.8 7.8 collective-permute-start.9
  735.5 13.5 %collective-permute-start.7 = (f32[32,256]{1,0:T(8,128)S(1)}, f32[32,256]{1,0:T(8,128)S(1)}, u32[]{:S(2)}, u32[]{:S(2)}) collective-permute-start(f32[32,256]{1,0:T(8,128)S(1)} %fusion), channel_id=1, source_target_pairs={{0,8},{1,9},{2,10},{3,11},{4,12},{5,13},{6,14},{7,15},{8,16},{9,17... | collective-permute-start | bytes 98312
  749.0 27.9 %collective-permute-start.6 = (f32[32,256]{1,0:T(8,128)S(1)}, f32[32,256]{1,0:T(8,128)S(1)}, u32[]{:S(2)}, u32[]{:S(2)}) collective-permute-start(f32[32,256]{1,0:T(8,128)S(1)} %fusion), channel_id=1, source_target_pairs={{0,7},{1,8},{2,9},{3,10},{4,11},{5,12},{6,13},{7,14},{8,15},{9,16}... | collective-permute-start | bytes 98312
  776.9 24.3 %collective-permute-start.5 = (f32[32,256]{1,0:T(8,128)S(1)}, f32[32,256]{1,0:T(8,128)S(1)}, u32[]{:S(2)}, u32[]{:S(2)}) collective-permute-start(f32[32,256]{1,0:T(8,128)S(1)} %fusion), channel_id=1, source_target_pairs={{0,6},{1,7},{2,8},{3,9},{4,10},{5,11},{6,12},{7,13},{8,14},{9,15},... | collective-permute-start | bytes 98312
  801.3 16.5 %collective-permute-start.4 = (f32[32,256]{1,0:T(8,128)S(1)}, f32[32,256]{1,0:T(8,128)S(1)}, u32[]{:S(2)}, u32[]{:S(2)}) collective-permute-start(f32[32,256]{1,0:T(8,128)S(1)} %fusion), channel_id=1, source_target_pairs={{0,5},{1,6},{2,7},{3,8},{4,9},{5,10},{6,11},{7,12},{8,13},{9,14},{... | collective-permute-start | bytes 98312
  817.8 3.0 collective-permute-start.3
  820.8 8.7 %collective-permute-start.2 = (f32[32,256]{1,0:T(8,128)S(1)}, f32[32,256]{1,0:T(8,128)S(1)}, u32[]{:S(2)}, u32[]{:S(2)}) collective-permute-start(f32[32,256]{1,0:T(8,128)S(1)} %fusion), channel_id=1, source_target_pairs={{0,3},{1,4},{2,5},{3,6},{4,7},{5,8},{6,9},{7,10},{8,11},{9,12},{10... | collective-permute-start | bytes 98312
  829.5 3.0 collective-permute-start.1
  834.5 3.7 collective-permute-done.2
  839.6 2.5 collective-permute-done
  842.0 2.1 concatenate.16
  (69 shorter events, 15.7 us)
Async XLA Ops:
  7.2 20.0 %copy-start.3 = (s32[1,1,1024]{2,1,0:T(1,128)S(1)}, s32[1,1,1024]{2,1,0:T(1,128)}, u32[]{:S(2)}) copy-start(s32[1,1,1024]{2,1,0:T(1,128)} %param.15) | copy-start | bytes 12292
  7.2 20.0 %copy-start.4 = (s32[1,1,1024]{2,1,0:T(1,128)S(1)}, s32[1,1,1024]{2,1,0:T(1,128)}, u32[]{:S(2)}) copy-start(s32[1,1,1024]{2,1,0:T(1,128)} %param.13) | copy-start | bytes 12292
  7.2 20.1 %copy-start.5 = (s32[1,1,1024]{2,1,0:T(1,128)S(1)}, s32[1,1,1024]{2,1,0:T(1,128)}, u32[]{:S(2)}) copy-start(s32[1,1,1024]{2,1,0:T(1,128)} %param.14) | copy-start | bytes 12292
  7.2 20.1 %copy-start.6 = (f32[1,1,1024]{2,1,0:T(1,128)S(1)}, f32[1,1,1024]{2,1,0:T(1,128)}, u32[]{:S(2)}) copy-start(f32[1,1,1024]{2,1,0:T(1,128)} %param.16) | copy-start | bytes 12292
  7.2 20.1 %copy-start.7 = (s32[1,1,8]{2,1,0:T(1,128)S(1)}, s32[1,1,8]{2,1,0:T(1,128)}, u32[]{:S(2)}) copy-start(s32[1,1,8]{2,1,0:T(1,128)} %param.17) | copy-start | bytes 100
  7.2 48.6 %all-gather.2.cloned.1.call-start = ((), (), s32[]{:S(2)}) async-start(), calls=%async_computation.3 | async-start | bytes 2228224 | tf_op jit(solution)/shard_map/all_gather | solution.py:20
  10.4 60.3 %all-to-all-start = ((bf16[16,256,256]{2,1,0:T(8,128)(2,1)}), bf16[16,256,256]{2,1,0:T(8,128)(2,1)S(1)}, u32[]{:S(2)}, u32[]{:S(2)}) async-start(bf16[16,256,256]{2,1,0:T(8,128)(2,1)} %stack.3), calls=%async_computation | async-start | bytes 4194304 | tf_op jit(solution)/shard_map/all_to_all | solution.py:12
  21.8 822.9 %all-reduce.4.cloned.1.call-start = ((), (), s32[]{:S(2)}) async-start(), calls=%async_computation.4 | async-start | bytes 2048000 | tf_op jit(solution)/shard_map/psum | solution.py:70
  74.8 5.5 copy-start
  74.8 5.5 copy-start.2
  74.9 5.5 copy-start.8
  91.1 756.0 %reduce-scatter.4.cloned.1.call-start = ((), (), s32[]{:S(2)}) async-start(), calls=%async_computation.2 | async-start | bytes 4456448 | tf_op jit(solution)/shard_map/reduce_scatter | solution.py:56
  100.1 4.2 copy-start.1
  708.1 9.6 %collective-permute-start.15 = (f32[30,256]{1,0:T(8,128)S(1)}, f32[30,256]{1,0:T(8,128)S(1)}, u32[]{:S(2)}, u32[]{:S(2)}) collective-permute-start(f32[30,256]{1,0:T(8,128)S(1)} %slice.56), channel_id=1, source_target_pairs={{0,16},{1,17},{2,18},{3,19},{4,20},{5,21},{6,22},{7,23},{8,24},{9,... | collective-permute-start | bytes 92168
  710.0 15.7 %collective-permute-start.14 = (f32[32,256]{1,0:T(8,128)S(1)}, f32[32,256]{1,0:T(8,128)S(1)}, u32[]{:S(2)}, u32[]{:S(2)}) collective-permute-start(f32[32,256]{1,0:T(8,128)S(1)} %fusion), channel_id=1, source_target_pairs={{0,15},{1,16},{2,17},{3,18},{4,19},{5,20},{6,21},{7,22},{8,23},{9,... | collective-permute-start | bytes 98312
  712.0 21.6 %collective-permute-start.13 = (f32[32,256]{1,0:T(8,128)S(1)}, f32[32,256]{1,0:T(8,128)S(1)}, u32[]{:S(2)}, u32[]{:S(2)}) collective-permute-start(f32[32,256]{1,0:T(8,128)S(1)} %fusion), channel_id=1, source_target_pairs={{0,14},{1,15},{2,16},{3,17},{4,18},{5,19},{6,20},{7,21},{8,22},{9,... | collective-permute-start | bytes 98312
  713.9 21.6 %collective-permute-start.12 = (f32[32,256]{1,0:T(8,128)S(1)}, f32[32,256]{1,0:T(8,128)S(1)}, u32[]{:S(2)}, u32[]{:S(2)}) collective-permute-start(f32[32,256]{1,0:T(8,128)S(1)} %fusion), channel_id=1, source_target_pairs={{0,13},{1,14},{2,15},{3,16},{4,17},{5,18},{6,19},{7,20},{8,21},{9,... | collective-permute-start | bytes 98312
  715.8 33.2 %collective-permute-start.11 = (f32[32,256]{1,0:T(8,128)S(1)}, f32[32,256]{1,0:T(8,128)S(1)}, u32[]{:S(2)}, u32[]{:S(2)}) collective-permute-start(f32[32,256]{1,0:T(8,128)S(1)} %fusion), channel_id=1, source_target_pairs={{0,12},{1,13},{2,14},{3,15},{4,16},{5,17},{6,18},{7,19},{8,20},{9,... | collective-permute-start | bytes 98312
  717.8 59.2 %collective-permute-start.10 = (f32[32,256]{1,0:T(8,128)S(1)}, f32[32,256]{1,0:T(8,128)S(1)}, u32[]{:S(2)}, u32[]{:S(2)}) collective-permute-start(f32[32,256]{1,0:T(8,128)S(1)} %fusion), channel_id=1, source_target_pairs={{0,11},{1,12},{2,13},{3,14},{4,15},{5,16},{6,17},{7,18},{8,19},{9,... | collective-permute-start | bytes 98312
  725.8 75.5 %collective-permute-start.9 = (f32[32,256]{1,0:T(8,128)S(1)}, f32[32,256]{1,0:T(8,128)S(1)}, u32[]{:S(2)}, u32[]{:S(2)}) collective-permute-start(f32[32,256]{1,0:T(8,128)S(1)} %fusion), channel_id=1, source_target_pairs={{0,10},{1,11},{2,12},{3,13},{4,14},{5,15},{6,16},{7,17},{8,18},{9,... | collective-permute-start | bytes 98312
  733.6 84.2 %collective-permute-start.8 = (f32[32,256]{1,0:T(8,128)S(1)}, f32[32,256]{1,0:T(8,128)S(1)}, u32[]{:S(2)}, u32[]{:S(2)}) collective-permute-start(f32[32,256]{1,0:T(8,128)S(1)} %fusion), channel_id=1, source_target_pairs={{0,9},{1,10},{2,11},{3,12},{4,13},{5,14},{6,15},{7,16},{8,17},{9,1... | collective-permute-start | bytes 98312
  735.5 85.3 %collective-permute-start.7 = (f32[32,256]{1,0:T(8,128)S(1)}, f32[32,256]{1,0:T(8,128)S(1)}, u32[]{:S(2)}, u32[]{:S(2)}) collective-permute-start(f32[32,256]{1,0:T(8,128)S(1)} %fusion), channel_id=1, source_target_pairs={{0,8},{1,9},{2,10},{3,11},{4,12},{5,13},{6,14},{7,15},{8,16},{9,17... | collective-permute-start | bytes 98312
  749.0 80.5 %collective-permute-start.6 = (f32[32,256]{1,0:T(8,128)S(1)}, f32[32,256]{1,0:T(8,128)S(1)}, u32[]{:S(2)}, u32[]{:S(2)}) collective-permute-start(f32[32,256]{1,0:T(8,128)S(1)} %fusion), channel_id=1, source_target_pairs={{0,7},{1,8},{2,9},{3,10},{4,11},{5,12},{6,13},{7,14},{8,15},{9,16}... | collective-permute-start | bytes 98312
  776.9 55.6 %collective-permute-start.5 = (f32[32,256]{1,0:T(8,128)S(1)}, f32[32,256]{1,0:T(8,128)S(1)}, u32[]{:S(2)}, u32[]{:S(2)}) collective-permute-start(f32[32,256]{1,0:T(8,128)S(1)} %fusion), channel_id=1, source_target_pairs={{0,6},{1,7},{2,8},{3,9},{4,10},{5,11},{6,12},{7,13},{8,14},{9,15},... | collective-permute-start | bytes 98312
  801.3 33.2 %collective-permute-start.4 = (f32[32,256]{1,0:T(8,128)S(1)}, f32[32,256]{1,0:T(8,128)S(1)}, u32[]{:S(2)}, u32[]{:S(2)}) collective-permute-start(f32[32,256]{1,0:T(8,128)S(1)} %fusion), channel_id=1, source_target_pairs={{0,5},{1,6},{2,7},{3,8},{4,9},{5,10},{6,11},{7,12},{8,13},{9,14},{... | collective-permute-start | bytes 98312
  817.8 16.7 %collective-permute-start.3 = (f32[32,256]{1,0:T(8,128)S(1)}, f32[32,256]{1,0:T(8,128)S(1)}, u32[]{:S(2)}, u32[]{:S(2)}) collective-permute-start(f32[32,256]{1,0:T(8,128)S(1)} %fusion), channel_id=1, source_target_pairs={{0,4},{1,5},{2,6},{3,7},{4,8},{5,9},{6,10},{7,11},{8,12},{9,13},{1... | collective-permute-start | bytes 98312
  820.8 17.5 %collective-permute-start.2 = (f32[32,256]{1,0:T(8,128)S(1)}, f32[32,256]{1,0:T(8,128)S(1)}, u32[]{:S(2)}, u32[]{:S(2)}) collective-permute-start(f32[32,256]{1,0:T(8,128)S(1)} %fusion), channel_id=1, source_target_pairs={{0,3},{1,4},{2,5},{3,6},{4,7},{5,8},{6,9},{7,10},{8,11},{9,12},{10... | collective-permute-start | bytes 98312
  829.5 10.0 %collective-permute-start.1 = (f32[32,256]{1,0:T(8,128)S(1)}, f32[32,256]{1,0:T(8,128)S(1)}, u32[]{:S(2)}, u32[]{:S(2)}) collective-permute-start(f32[32,256]{1,0:T(8,128)S(1)} %fusion), channel_id=1, source_target_pairs={{0,2},{1,3},{2,4},{3,5},{4,6},{5,7},{6,8},{7,9},{8,10},{9,11},{10,... | collective-permute-start | bytes 98312
  832.6 9.5 %collective-permute-start = (f32[32,256]{1,0:T(8,128)S(1)}, f32[32,256]{1,0:T(8,128)S(1)}, u32[]{:S(2)}, u32[]{:S(2)}) collective-permute-start(f32[32,256]{1,0:T(8,128)S(1)} %fusion), channel_id=1, source_target_pairs={{0,1},{1,2},{2,3},{3,4},{4,5},{5,6},{6,7},{7,8},{8,9},{9,10},{10,1... | collective-permute-start | bytes 98312
Sparse Core Ops, SparseCore 0:
  9.9 45.9 all-gather.1
  91.2 260.6 all-reduce.3
  354.5 73.7 reduce-scatter.3
